TPU v7x, 32 devices: a whole 2x2x4 slice. The times are simulated.
32 devices in a mesh: stn: 2 (over x), vox: 16 (over z, y, core).
Axes of the slice: x: 2, y: 2, z: 4, core: 2. Of those that a mesh axis runs over, the one named last changes fastest.
Arguments:
- voltages: bfloat16 [56, 2, 65536], P('stn', None, 'vox'), may hold values from -6 to 6
- sample_delays: int32 [56, 65536], P(None, 'vox'), may hold values from 0 to 239
- timing_offsets: int32 [56], replicated, may hold values from 0 to 15
- reference_station: int32 [1], replicated, may hold values from 0 to 55
Outputs:
- image_out: float32 [64, 65536], P('stn', 'vox')
All inputs are finite; a program needn't handle non-finite values.
Results may differ from a plain program's by a relative error of at most 0.004.
Values may be sent and summed in bfloat16 or wider, within the bound.
No kernel may reach another device: no remote copies, remote signals or barrier semaphores. Data moves between devices by JAX's collectives and lax.ppermute only.
A program may use at most 64 MiB of HBM per device.

v0:
```python
import math
import jax
import jax.numpy as jnp
from jax import lax
from jax.sharding import PartitionSpec as P

STATIONS = 56
WIN = 1024
LAGS = 256


def spread(value, axis, source):
    kept = jnp.where(lax.axis_index(axis) == source, value, 0).astype(value.dtype)
    return lax.psum(kept, axis)


def padded(block, sides, width):
    for axis, dim in sides:
        count = lax.axis_size(axis)
        forward = [(i, i + 1) for i in range(count - 1)]
        backward = [(target, source) for source, target in forward]
        low = lax.ppermute(
            lax.slice_in_dim(block, block.shape[dim] - width, None, axis=dim), axis, forward
        )
        high = lax.ppermute(lax.slice_in_dim(block, 0, width, axis=dim), axis, backward)
        block = jnp.concatenate([low, block, high], axis=dim)
    return block


def taper_weights(length):
    position = (jnp.arange(length, dtype=jnp.float32) + 0.5) / length
    return 0.5 - 0.5 * jnp.cos(2.0 * math.pi * position)


def shards(voltages, sample_delays, timing_offsets, reference_station):
    stations_here, polarizations, samples_here = voltages.shape
    slices_here = samples_here // WIN
    voxels_here = sample_delays.shape[1]
    station_ref = reference_station[0]
    stn_index = lax.axis_index("stn")
    taper_curve = taper_weights(WIN)
    norm_inv = 1.0 / jnp.sqrt(jnp.sum(taper_curve * taper_curve))
    owner_index = station_ref // stations_here
    ref_local = lax.dynamic_index_in_dim(voltages, station_ref % stations_here, 0, keepdims=False)
    ref_signal = spread(ref_local, "stn", owner_index)
    extended = padded(ref_signal, (("vox", 1),), LAGS // 2)
    extended = jnp.pad(extended, ((0, 0), (0, WIN)))
    leading = extended[:, :samples_here].reshape(polarizations, slices_here, WIN)
    trailing = extended[:, WIN : samples_here + WIN].reshape(polarizations, slices_here, WIN)[
        :, :, : LAGS - 1
    ]
    segments = jnp.concatenate([leading, trailing], axis=2).reshape(
        1, polarizations * slices_here, WIN + LAGS - 1
    )
    windowed = (
        voltages.reshape(stations_here, polarizations, slices_here, WIN) * taper_curve
    ).astype(jnp.bfloat16)
    kernels = jnp.transpose(windowed, (1, 2, 0, 3)).reshape(
        polarizations * slices_here * stations_here, 1, WIN
    )
    lagged_sums = lax.conv_general_dilated(
        segments,
        kernels,
        (1,),
        "VALID",
        feature_group_count=polarizations * slices_here,
        preferred_element_type=jnp.float32,
    )
    lagged_sums = jnp.sum(
        lagged_sums.reshape(polarizations, slices_here, stations_here, LAGS), axis=0
    )
    station_ids = stn_index * stations_here + jnp.arange(stations_here, dtype=jnp.int32)
    keep_mask = (station_ids != station_ref).astype(jnp.float32)
    local_corr = (
        jnp.transpose(lagged_sums, (1, 0, 2)) * keep_mask[:, None, None] * norm_inv
    ).astype(jnp.bfloat16)
    corr_all = lax.all_gather(local_corr, "vox", axis=1, tiled=True)
    lag_index = sample_delays + timing_offsets[:, None]
    total_slices = corr_all.shape[1]
    out_scale = 1.0 / math.sqrt(2.0 * STATIONS)
    my_lags = lax.dynamic_slice_in_dim(lag_index, stn_index * stations_here, stations_here, 0)
    corr_block = lax.slice_in_dim(
        corr_all, 0, lax.axis_size("stn") * (total_slices // lax.axis_size("stn")), axis=1
    )
    lag_grid = lax.broadcasted_iota(jnp.int32, (LAGS, voxels_here), 0)

    def add_station(running, inputs_pair):
        corr_rows, lags_one = inputs_pair
        selector = (lag_grid == lags_one[None, :]).astype(jnp.bfloat16)
        return (running + jnp.dot(corr_rows, selector, preferred_element_type=jnp.float32), None)

    running, unused = lax.scan(
        add_station,
        jnp.zeros(
            (lax.axis_size("stn") * (total_slices // lax.axis_size("stn")), voxels_here),
            jnp.float32,
        ),
        (corr_block, my_lags),
    )
    image_out = lax.psum_scatter(running, "stn", scatter_dimension=0, tiled=True)
    return image_out * out_scale


def solution(mesh):
    return jax.shard_map(
        shards,
        mesh=mesh,
        in_specs=(P("stn", None, "vox"), P(None, "vox"), P(), P()),
        out_specs=P("stn", "vox"),
        check_vma=False,
    )
```

profile of v0, /device:TPU:0, one launch (start us, length us, event | category | flops | bytes accessed | tf_op | source)
XLA Modules:
  0.0 126.3 jit_solution(5938789996437528588)
XLA Ops:
  8.0 9.7 %psum.7 = bf16[2,4096]{1,0:T(2,128)(2,1)S(1)} all-reduce(bf16[2,4096]{1,0:T(2,128)(2,1)S(1)} %fusion.14), channel_id=1, replica_groups=mesh['stn'=2,'vox'=16] {'stn'}, use_global_device_ids=true, to_apply=%region_0.0 | all-reduce | flops 8192 | bytes 32768 | tf_op jit(solution)/shard_map/psum | solution.py:14
  17.6 1.3 %collective-permute-start = (bf16[2,128]{1,0:T(2,128)(2,1)S(1)}, bf16[2,128]{1,0:T(2,128)(2,1)S(1)}, u32[]{:S(2)}, u32[]{:S(2)}) collective-permute-start(bf16[2,128]{1,0:T(2,128)(2,1)S(1)} %get-tuple-element.64), channel_id=1, source_target_pairs={{0,1},{1,2},{2,3},{3,4},{4,5},{5,6},{6,7},{7,8},{8,9},{9,10},{10,1... | collective-permute-start | bytes 1544 | tf_op jit(solution)/shard_map/ppermute | solution.py:22
  18.9 1.3 %collective-permute-start.1 = (bf16[2,128]{1,0:T(2,128)(2,1)S(1)}, bf16[2,128]{1,0:T(2,128)(2,1)S(1)}, u32[]{:S(2)}, u32[]{:S(2)}) collective-permute-start(bf16[2,128]{1,0:T(2,128)(2,1)S(1)} %get-tuple-element.65), channel_id=1, source_target_pairs={{1,0},{2,1},{3,2},{4,3},{5,4},{6,5},{7,6},{8,7},{9,8},{10,9},{11,1... | collective-permute-start | bytes 1544 | tf_op jit(solution)/shard_map/ppermute | solution.py:25
  20.2 1.4 %reshape.40 = f32[28,2,4,1024]{3,2,1,0:T(4,128)S(1)} reshape(bf16[28,2,4096]{2,1,0:T(2,128)(2,1)} %param.6) | data formatting | bytes 1376256 | tf_op jit(solution)/shard_map/convert_element_type | solution.py:56
  25.6 16.9 %fusion.7 = f32[1,224,256]{1,0,2:T(1,128)S(1)} fusion(bf16[1,8,1279]{1,0,2:T(2,128)(2,1)S(1)} %copy.13, s32[224]{0:T(256)S(1)} %copy-done.3, bf16[224,1024]{0,1:T(8,128)(2,1)S(1)} %copy.12), kind=kOutput, calls=%fused_computation.10 | convolution fusion | flops 943194112 | bytes 709488 | tf_op jit(solution)/shard_map/conv_general_dilated | solution.py:61
  42.8 27.5 %all_gather.3 = bf16[28,64,256]{2,0,1:T(8,128)(2,1)S(1)} all-gather(bf16[28,4,256]{2,0,1:T(8,128)(2,1)S(1)} %fusion.13), channel_id=1, replica_groups=mesh['stn'=2,'vox'=16] {'vox'}, dimensions={1}, use_global_device_ids=true | all-gather | bytes 974848 | tf_op jit(solution)/shard_map/all_gather | solution.py:77
  70.9 28.9 %while.11 = (s32[]{:T(128)}, f32[64,4096]{1,0:T(8,128)S(1)}, bf16[28,64,256]{2,1,0:T(8,128)(2,1)S(1)}, s32[28,4096]{1,0:T(8,128)S(1)}, s32[]{:T(128)}, /*index=5*/s32[]{:T(128)}) while((s32[]{:T(128)}, f32[64,4096]{1,0:T(8,128)S(1)}, bf16[28,64,256]{2,1,0:T(8,128)(2,1)S(1)}, s32[28,4096]{1,0:T(8,128)S(1)}, s32[]{:T(128)}, ...), condition=%wide.region_4.5_spmd.clone, body=%wide.region_3.4_spmd.clone.sunk | while | flops 135790592 | bytes 2179159 | solution.py:92
  70.9 1.0 convolution_add_fusion.2
  73.0 1.0 convolution_add_fusion.2
  75.1 1.0 convolution_add_fusion.2
  77.1 1.0 convolution_add_fusion.2
  79.2 1.0 convolution_add_fusion.2
  81.2 1.0 convolution_add_fusion.2
  83.3 1.0 convolution_add_fusion.2
  85.4 1.0 convolution_add_fusion.2
  87.4 1.0 convolution_add_fusion.2
  89.5 1.0 convolution_add_fusion.2
  91.6 1.0 convolution_add_fusion.2
  93.6 1.0 convolution_add_fusion.2
  95.7 1.0 convolution_add_fusion.2
  97.7 1.0 convolution_add_fusion.2
  99.8 1.0 copy-done
  100.8 16.8 %reduce-scatter.2.cloned.1.call-done = f32[32,4096]{1,0:T(8,128)} async-done(((f32[64,4096]{1,0:T(8,128)}), f32[32,4096]{1,0:T(8,128)}) %reduce-scatter.2.cloned.1.call-update) | async-done | bytes 524304 | tf_op jit(solution)/shard_map/reduce_scatter | solution.py:100
  117.6 1.9 %broadcast_multiply_fusion = f32[32,4096]{1,0:T(8,128)} fusion(f32[32,4096]{1,0:T(8,128)} %reduce-scatter.2.cloned.1.call-done), kind=kLoop, calls=%fused_computation.17 | loop fusion | flops 131072 | bytes 1048576 | tf_op jit(solution)/shard_map/mul | solution.py:101
  (76 shorter events, 19.0 us)
Async XLA Ops:
  6.5 111.1 %reduce-scatter.2.cloned.1.call-start = ((), (), s32[]{:S(2)}) async-start(), calls=%async_computation.1 | async-start | bytes 1572864 | tf_op jit(solution)/shard_map/reduce_scatter | solution.py:100
  17.6 6.9 %collective-permute-start = (bf16[2,128]{1,0:T(2,128)(2,1)S(1)}, bf16[2,128]{1,0:T(2,128)(2,1)S(1)}, u32[]{:S(2)}, u32[]{:S(2)}) collective-permute-start(bf16[2,128]{1,0:T(2,128)(2,1)S(1)} %get-tuple-element.64), channel_id=1, source_target_pairs={{0,1},{1,2},{2,3},{3,4},{4,5},{5,6},{6,7},{7,8},{8,9},{9,10},{10,1... | collective-permute-start | bytes 1544 | tf_op jit(solution)/shard_map/ppermute | solution.py:22
  18.9 5.6 %collective-permute-start.1 = (bf16[2,128]{1,0:T(2,128)(2,1)S(1)}, bf16[2,128]{1,0:T(2,128)(2,1)S(1)}, u32[]{:S(2)}, u32[]{:S(2)}) collective-permute-start(bf16[2,128]{1,0:T(2,128)(2,1)S(1)} %get-tuple-element.65), channel_id=1, source_target_pairs={{1,0},{2,1},{3,2},{4,3},{5,4},{6,5},{7,6},{8,7},{9,8},{10,9},{11,1... | collective-permute-start | bytes 1544 | tf_op jit(solution)/shard_map/ppermute | solution.py:25
  21.7 0.7 copy-start.2
  21.7 1.2 copy-start.1
  23.1 2.5 %copy-start.3 = (s32[224]{0:T(256)S(1)}, s32[224]{0:T(256)}, u32[]{:S(2)}) copy-start(s32[224]{0:T(256)} %constant.54.clone.1) | copy-start | bytes 2692
  99.8 1.0 copy-start
Sparse Core Ops, SparseCore 0:
  100.9 16.6 reduce-scatter.1
where the time goes:
time: 127 us; the launch traced here: 126 us
  matrix products  44.3 us (35%)
  blocking collectives  37.2 us (29%)
  waiting for transfers between devices  16.8 us (13%)
  between operations  14.9 us (12%)
  local copies, waits for them, and re-layouts  5.49 us (4%)
  other arithmetic  4.06 us (3%)
  starting transfers between devices  2.58 us (2%)
    all_gather x1, blocking collectives, shards(): corr_all = lax.all_gather(local_corr, 'vox', axis=1, tiled=True)  27.5 us
    dot_general x28, matrix products, add_station(): jnp.dot(corr_rows, selector, preferred_element_type=jnp.float32)  27.4 us
    conv_general_dilated x1, matrix products, shards(): lax.conv_general_dilated(segments, kernels, (1,), 'VALID', feature_group_...  16.9 us
    reduce_scatter x1, waiting for transfers between devices, shards(): lax.psum_scatter(running, 'stn', scatter_dimension=0, tiled=True)  16.8 us
    psum x1, blocking collectives, spread(): return lax.psum(kept, axis)  9.65 us
  transfers between devices with their start and end apart: 3, of which 1 were waited for; matrix products, arithmetic and copies ran while one was open for 2% of the time, Pallas kernels for 0%

commit v1 on v0

--- a/solution.py
+++ b/solution.py
@@ -74,7 +74,18 @@
     local_corr = (
         jnp.transpose(lagged_sums, (1, 0, 2)) * keep_mask[:, None, None] * norm_inv
     ).astype(jnp.bfloat16)
-    corr_all = lax.all_gather(local_corr, "vox", axis=1, tiled=True)
+    dev_n = lax.axis_size("vox")
+    pile = tuple(((d, (d + 1) % dev_n) for d in range(dev_n)))
+    all_rows = tuple(((d, (d - 1) % dev_n) for d in range(dev_n)))
+    z2, g_now = ([local_corr], [local_corr])
+    for _ in range(dev_n // 2):
+        t_next = lax.ppermute(z2[-1], "vox", pile)
+        z2.append(t_next)
+    for _ in tuple(range((dev_n - 1) // 2)):
+        g_now.append(lax.ppermute(g_now[-1], "vox", all_rows))
+    f_next = jnp.concatenate([*z2[::-1], *g_now[1:]], 1)
+    part_now = lax.axis_index("vox")
+    corr_all = jnp.roll(f_next, (part_now - dev_n // 2) * local_corr.shape[1], axis=1)
     lag_index = sample_delays + timing_offsets[:, None]
     total_slices = corr_all.shape[1]
     out_scale = 1.0 / math.sqrt(2.0 * STATIONS)

time: 127 us -> 155 us (1.22)
  starting transfers between devices: 2.58 us -> 36.8 us
  blocking collectives: 37.2 us -> 9.65 us
  waiting for transfers between devices: 16.8 us -> 38.7 us
    ppermute x0 -> x15, starting transfers between devices: none -> 34.2 us  [the longest x7 31.3 us: shards(): g_now.append(lax.ppermute(g_now[-1], 'vox', all_rows))]
    all_gather x1 -> x0, blocking collectives: 27.5 us -> none  [shards(): corr_all = lax.all_gather(local_corr, 'vox', axis=1, tiled=True)]
    ppermute x0 -> x15, waiting for transfers between devices: none -> 18.1 us  [the longest x8 18 us: shards(): t_next = lax.ppermute(z2[-1], 'vox', pile)]
    reduce_scatter x1, waiting for transfers between devices: 16.8 us -> 20.6 us  [shards(): lax.psum_scatter(running, 'stn', scatter_dimension=0, tiled=True)]
  transfers between devices with their start and end apart: 3 -> 18, of which waited for: 1 -> 9; matrix products, arithmetic and copies ran while one was open for 2% -> 2% of each run, Pallas kernels for 0% -> 0%
where the time goes in v1:
time: 155 us
  matrix products  44.2 us (29%)
  waiting for transfers between devices  38.7 us (25%)
  starting transfers between devices  36.8 us (24%)
  between operations  15.3 us (10%)
  blocking collectives  9.65 us (6%)
  local copies, waits for them, and re-layouts  5.05 us (3%)
  other arithmetic  4.23 us (3%)
    ppermute x7, starting transfers between devices, shards(): g_now.append(lax.ppermute(g_now[-1], 'vox', all_rows))  31.3 us
    dot_general x28, matrix products, add_station(): jnp.dot(corr_rows, selector, preferred_element_type=jnp.float32)  27.4 us
    reduce_scatter x1, waiting for transfers between devices, shards(): lax.psum_scatter(running, 'stn', scatter_dimension=0, tiled=True)  20.6 us
    ppermute x8, waiting for transfers between devices, shards(): t_next = lax.ppermute(z2[-1], 'vox', pile)  18 us
    conv_general_dilated x1, matrix products, shards(): lax.conv_general_dilated(segments, kernels, (1,), 'VALID', feature_group_...  16.9 us
    psum x1, blocking collectives, spread(): return lax.psum(kept, axis)  9.65 us
  transfers between devices with their start and end apart: 18, of which 9 were waited for; matrix products, arithmetic and copies ran while one was open for 2% of the time, Pallas kernels for 0%

profile of v1, /device:TPU:0, one launch (start us, length us, event | category | flops | bytes accessed | tf_op | source)
XLA Modules:
  0.0 155.0 jit_solution(6300618414055516323)
XLA Ops:
  8.0 9.7 %psum.7 = bf16[2,4096]{1,0:T(2,128)(2,1)S(1)} all-reduce(bf16[2,4096]{1,0:T(2,128)(2,1)S(1)} %fusion.14), channel_id=1, replica_groups=mesh['stn'=2,'vox'=16] {'stn'}, use_global_device_ids=true, to_apply=%region_0.0 | all-reduce | flops 8192 | bytes 32768 | tf_op jit(solution)/shard_map/psum | solution.py:14
  17.6 1.3 collective-permute-start
  18.9 1.3 collective-permute-start.1
  20.2 1.4 reshape.40
  24.8 16.9 %fusion.7 = f32[1,224,256]{1,0,2:T(1,128)S(1)} fusion(bf16[1,8,1279]{1,0,2:T(2,128)(2,1)S(1)} %copy.13, s32[224]{0:T(256)S(1)} %copy-done.3, bf16[224,1024]{0,1:T(8,128)(2,1)S(1)} %copy.12), kind=kOutput, calls=%fused_computation.10 | convolution fusion | flops 943194112 | bytes 709488 | tf_op jit(solution)/shard_map/conv_general_dilated | solution.py:61
  42.0 2.9 %collective-permute-start.2 = (bf16[28,4,256]{2,0,1:T(8,128)(2,1)S(1)}, bf16[28,4,256]{2,0,1:T(8,128)(2,1)S(1)}, u32[]{:S(2)}, u32[]{:S(2)}) collective-permute-start(bf16[28,4,256]{2,0,1:T(8,128)(2,1)S(1)} %fusion.13), channel_id=1, source_target_pairs={{0,1},{1,2},{2,3},{3,4},{4,5},{5,6},{6,7},{7,8},{8,9},{9,10},{10,1... | collective-permute-start | bytes 172040 | tf_op jit(solution)/shard_map/ppermute | solution.py:82
  44.9 5.0 %collective-permute-done.2 = bf16[28,4,256]{2,0,1:T(8,128)(2,1)S(1)} collective-permute-done((bf16[28,4,256]{2,0,1:T(8,128)(2,1)S(1)}, bf16[28,4,256]{2,0,1:T(8,128)(2,1)S(1)}, u32[]{:S(2)}, u32[]{:S(2)}) %collective-permute-start.2) | collective-permute-done | bytes 57376 | tf_op jit(solution)/shard_map/ppermute | solution.py:82
  49.8 4.4 %collective-permute-start.10 = (bf16[28,4,256]{2,0,1:T(8,128)(2,1)S(1)}, bf16[28,4,256]{2,0,1:T(8,128)(2,1)S(1)}, u32[]{:S(2)}, u32[]{:S(2)}) collective-permute-start(bf16[28,4,256]{2,0,1:T(8,128)(2,1)S(1)} %fusion.13), channel_id=1, source_target_pairs={{0,15},{1,0},{2,1},{3,2},{4,3},{5,4},{6,5},{7,6},{8,7},{9,8},{10,9... | collective-permute-start | bytes 172040 | tf_op jit(solution)/shard_map/ppermute | solution.py:85
  54.3 1.9 %collective-permute-done.3 = bf16[28,4,256]{2,0,1:T(8,128)(2,1)S(1)} collective-permute-done((bf16[28,4,256]{2,0,1:T(8,128)(2,1)S(1)}, bf16[28,4,256]{2,0,1:T(8,128)(2,1)S(1)}, u32[]{:S(2)}, u32[]{:S(2)}) %collective-permute-start.3) | collective-permute-done | bytes 57376 | tf_op jit(solution)/shard_map/ppermute | solution.py:82
  56.2 4.5 %collective-permute-start.11 = (bf16[28,4,256]{2,0,1:T(8,128)(2,1)S(1)}, bf16[28,4,256]{2,0,1:T(8,128)(2,1)S(1)}, u32[]{:S(2)}, u32[]{:S(2)}) collective-permute-start(bf16[28,4,256]{2,0,1:T(8,128)(2,1)S(1)} %collective-permute-done.10), channel_id=1, source_target_pairs={{0,15},{1,0},{2,1},{3,2},{4,3},{5,4},{6,5},{7,6},{8,7},{9,8},{10,9... | collective-permute-start | bytes 172040 | tf_op jit(solution)/shard_map/ppermute | solution.py:85
  60.7 1.9 %collective-permute-done.4 = bf16[28,4,256]{2,0,1:T(8,128)(2,1)S(1)} collective-permute-done((bf16[28,4,256]{2,0,1:T(8,128)(2,1)S(1)}, bf16[28,4,256]{2,0,1:T(8,128)(2,1)S(1)}, u32[]{:S(2)}, u32[]{:S(2)}) %collective-permute-start.4) | collective-permute-done | bytes 57376 | tf_op jit(solution)/shard_map/ppermute | solution.py:82
  62.6 4.5 %collective-permute-start.12 = (bf16[28,4,256]{2,0,1:T(8,128)(2,1)S(1)}, bf16[28,4,256]{2,0,1:T(8,128)(2,1)S(1)}, u32[]{:S(2)}, u32[]{:S(2)}) collective-permute-start(bf16[28,4,256]{2,0,1:T(8,128)(2,1)S(1)} %collective-permute-done.11), channel_id=1, source_target_pairs={{0,15},{1,0},{2,1},{3,2},{4,3},{5,4},{6,5},{7,6},{8,7},{9,8},{10,9... | collective-permute-start | bytes 172040 | tf_op jit(solution)/shard_map/ppermute | solution.py:85
  67.1 1.9 %collective-permute-done.5 = bf16[28,4,256]{2,0,1:T(8,128)(2,1)S(1)} collective-permute-done((bf16[28,4,256]{2,0,1:T(8,128)(2,1)S(1)}, bf16[28,4,256]{2,0,1:T(8,128)(2,1)S(1)}, u32[]{:S(2)}, u32[]{:S(2)}) %collective-permute-start.5) | collective-permute-done | bytes 57376 | tf_op jit(solution)/shard_map/ppermute | solution.py:82
  69.0 4.5 %collective-permute-start.13 = (bf16[28,4,256]{2,0,1:T(8,128)(2,1)S(1)}, bf16[28,4,256]{2,0,1:T(8,128)(2,1)S(1)}, u32[]{:S(2)}, u32[]{:S(2)}) collective-permute-start(bf16[28,4,256]{2,0,1:T(8,128)(2,1)S(1)} %collective-permute-done.12), channel_id=1, source_target_pairs={{0,15},{1,0},{2,1},{3,2},{4,3},{5,4},{6,5},{7,6},{8,7},{9,8},{10,9... | collective-permute-start | bytes 172040 | tf_op jit(solution)/shard_map/ppermute | solution.py:85
  73.5 1.9 %collective-permute-done.6 = bf16[28,4,256]{2,0,1:T(8,128)(2,1)S(1)} collective-permute-done((bf16[28,4,256]{2,0,1:T(8,128)(2,1)S(1)}, bf16[28,4,256]{2,0,1:T(8,128)(2,1)S(1)}, u32[]{:S(2)}, u32[]{:S(2)}) %collective-permute-start.6) | collective-permute-done | bytes 57376 | tf_op jit(solution)/shard_map/ppermute | solution.py:82
  75.4 4.5 %collective-permute-start.14 = (bf16[28,4,256]{2,0,1:T(8,128)(2,1)S(1)}, bf16[28,4,256]{2,0,1:T(8,128)(2,1)S(1)}, u32[]{:S(2)}, u32[]{:S(2)}) collective-permute-start(bf16[28,4,256]{2,0,1:T(8,128)(2,1)S(1)} %collective-permute-done.13), channel_id=1, source_target_pairs={{0,15},{1,0},{2,1},{3,2},{4,3},{5,4},{6,5},{7,6},{8,7},{9,8},{10,9... | collective-permute-start | bytes 172040 | tf_op jit(solution)/shard_map/ppermute | solution.py:85
  79.9 1.9 %collective-permute-done.7 = bf16[28,4,256]{2,0,1:T(8,128)(2,1)S(1)} collective-permute-done((bf16[28,4,256]{2,0,1:T(8,128)(2,1)S(1)}, bf16[28,4,256]{2,0,1:T(8,128)(2,1)S(1)}, u32[]{:S(2)}, u32[]{:S(2)}) %collective-permute-start.7) | collective-permute-done | bytes 57376 | tf_op jit(solution)/shard_map/ppermute | solution.py:82
  81.9 4.4 %collective-permute-start.15 = (bf16[28,4,256]{2,0,1:T(8,128)(2,1)S(1)}, bf16[28,4,256]{2,0,1:T(8,128)(2,1)S(1)}, u32[]{:S(2)}, u32[]{:S(2)}) collective-permute-start(bf16[28,4,256]{2,0,1:T(8,128)(2,1)S(1)} %collective-permute-done.14), channel_id=1, source_target_pairs={{0,15},{1,0},{2,1},{3,2},{4,3},{5,4},{6,5},{7,6},{8,7},{9,8},{10,9... | collective-permute-start | bytes 172040 | tf_op jit(solution)/shard_map/ppermute | solution.py:85
  86.3 1.9 %collective-permute-done.8 = bf16[28,4,256]{2,0,1:T(8,128)(2,1)S(1)} collective-permute-done((bf16[28,4,256]{2,0,1:T(8,128)(2,1)S(1)}, bf16[28,4,256]{2,0,1:T(8,128)(2,1)S(1)}, u32[]{:S(2)}, u32[]{:S(2)}) %collective-permute-start.8) | collective-permute-done | bytes 57376 | tf_op jit(solution)/shard_map/ppermute | solution.py:82
  88.3 4.5 %collective-permute-start.16 = (bf16[28,4,256]{2,0,1:T(8,128)(2,1)S(1)}, bf16[28,4,256]{2,0,1:T(8,128)(2,1)S(1)}, u32[]{:S(2)}, u32[]{:S(2)}) collective-permute-start(bf16[28,4,256]{2,0,1:T(8,128)(2,1)S(1)} %collective-permute-done.15), channel_id=1, source_target_pairs={{0,15},{1,0},{2,1},{3,2},{4,3},{5,4},{6,5},{7,6},{8,7},{9,8},{10,9... | collective-permute-start | bytes 172040 | tf_op jit(solution)/shard_map/ppermute | solution.py:85
  92.8 1.7 %collective-permute-done.9 = bf16[28,4,256]{2,0,1:T(8,128)(2,1)S(1)} collective-permute-done((bf16[28,4,256]{2,0,1:T(8,128)(2,1)S(1)}, bf16[28,4,256]{2,0,1:T(8,128)(2,1)S(1)}, u32[]{:S(2)}, u32[]{:S(2)}) %collective-permute-start.9) | collective-permute-done | bytes 57376 | tf_op jit(solution)/shard_map/ppermute | solution.py:82
  95.8 28.9 %while.11 = (s32[]{:T(128)}, f32[64,4096]{1,0:T(8,128)S(1)}, bf16[28,64,256]{2,1,0:T(8,128)(2,1)S(1)}, s32[28,4096]{1,0:T(8,128)S(1)}, s32[]{:T(128)}, /*index=5*/s32[]{:T(128)}) while((s32[]{:T(128)}, f32[64,4096]{1,0:T(8,128)S(1)}, bf16[28,64,256]{2,1,0:T(8,128)(2,1)S(1)}, s32[28,4096]{1,0:T(8,128)S(1)}, s32[]{:T(128)}, ...), condition=%wide.region_4.5_spmd.clone, body=%wide.region_3.4_spmd.clone.sunk | while | flops 135790592 | bytes 2179159 | solution.py:103
  125.7 20.6 %reduce-scatter.2.cloned.1.call-done = f32[32,4096]{1,0:T(8,128)} async-done(((f32[64,4096]{1,0:T(8,128)}), f32[32,4096]{1,0:T(8,128)}) %reduce-scatter.2.cloned.1.call-update) | async-done | bytes 524304 | tf_op jit(solution)/shard_map/reduce_scatter | solution.py:111
  146.3 1.9 %broadcast_multiply_fusion = f32[32,4096]{1,0:T(8,128)} fusion(f32[32,4096]{1,0:T(8,128)} %reduce-scatter.2.cloned.1.call-done), kind=kLoop, calls=%fused_computation.17 | loop fusion | flops 131072 | bytes 1048576 | tf_op jit(solution)/shard_map/mul | solution.py:112
  (138 shorter events, 33.5 us)
Async XLA Ops:
  6.5 139.8 %reduce-scatter.2.cloned.1.call-start = ((), (), s32[]{:S(2)}) async-start(), calls=%async_computation.1 | async-start | bytes 1572864 | tf_op jit(solution)/shard_map/reduce_scatter | solution.py:111
  17.6 6.3 %collective-permute-start = (bf16[2,128]{1,0:T(2,128)(2,1)S(1)}, bf16[2,128]{1,0:T(2,128)(2,1)S(1)}, u32[]{:S(2)}, u32[]{:S(2)}) collective-permute-start(bf16[2,128]{1,0:T(2,128)(2,1)S(1)} %get-tuple-element.64), channel_id=1, source_target_pairs={{0,1},{1,2},{2,3},{3,4},{4,5},{5,6},{6,7},{7,8},{8,9},{9,10},{10,1... | collective-permute-start | bytes 1544 | tf_op jit(solution)/shard_map/ppermute | solution.py:22
  18.9 5.0 %collective-permute-start.1 = (bf16[2,128]{1,0:T(2,128)(2,1)S(1)}, bf16[2,128]{1,0:T(2,128)(2,1)S(1)}, u32[]{:S(2)}, u32[]{:S(2)}) collective-permute-start(bf16[2,128]{1,0:T(2,128)(2,1)S(1)} %get-tuple-element.65), channel_id=1, source_target_pairs={{1,0},{2,1},{3,2},{4,3},{5,4},{6,5},{7,6},{8,7},{9,8},{10,9},{11,1... | collective-permute-start | bytes 1544 | tf_op jit(solution)/shard_map/ppermute | solution.py:25
  21.7 3.1 %copy-start.3 = (s32[224]{0:T(256)S(1)}, s32[224]{0:T(256)}, u32[]{:S(2)}) copy-start(s32[224]{0:T(256)} %constant.77.clone.1) | copy-start | bytes 2692
  24.8 57.0 %copy-start.2 = (s32[56]{0:T(128)S(1)}, s32[56]{0:T(128)}, u32[]{:S(2)}) copy-start(s32[56]{0:T(128)} %param.8) | copy-start | bytes 676
  24.8 63.4 %copy-start.1 = (s32[56,4096]{1,0:T(8,128)S(1)}, s32[56,4096]{1,0:T(8,128)}, u32[]{:S(2)}) copy-start(s32[56,4096]{1,0:T(8,128)} %param.7) | copy-start | bytes 2752516
  42.0 7.9 %collective-permute-start.2 = (bf16[28,4,256]{2,0,1:T(8,128)(2,1)S(1)}, bf16[28,4,256]{2,0,1:T(8,128)(2,1)S(1)}, u32[]{:S(2)}, u32[]{:S(2)}) collective-permute-start(bf16[28,4,256]{2,0,1:T(8,128)(2,1)S(1)} %fusion.13), channel_id=1, source_target_pairs={{0,1},{1,2},{2,3},{3,4},{4,5},{5,6},{6,7},{7,8},{8,9},{9,10},{10,1... | collective-permute-start | bytes 172040 | tf_op jit(solution)/shard_map/ppermute | solution.py:82
  49.8 6.4 %collective-permute-start.3 = (bf16[28,4,256]{2,0,1:T(8,128)(2,1)S(1)}, bf16[28,4,256]{2,0,1:T(8,128)(2,1)S(1)}, u32[]{:S(2)}, u32[]{:S(2)}) collective-permute-start(bf16[28,4,256]{2,0,1:T(8,128)(2,1)S(1)} %collective-permute-done.2), channel_id=1, source_target_pairs={{0,1},{1,2},{2,3},{3,4},{4,5},{5,6},{6,7},{7,8},{8,9},{9,10},{10,1... | collective-permute-start | bytes 172040 | tf_op jit(solution)/shard_map/ppermute | solution.py:82
  49.8 6.4 %collective-permute-start.10 = (bf16[28,4,256]{2,0,1:T(8,128)(2,1)S(1)}, bf16[28,4,256]{2,0,1:T(8,128)(2,1)S(1)}, u32[]{:S(2)}, u32[]{:S(2)}) collective-permute-start(bf16[28,4,256]{2,0,1:T(8,128)(2,1)S(1)} %fusion.13), channel_id=1, source_target_pairs={{0,15},{1,0},{2,1},{3,2},{4,3},{5,4},{6,5},{7,6},{8,7},{9,8},{10,9... | collective-permute-start | bytes 172040 | tf_op jit(solution)/shard_map/ppermute | solution.py:85
  56.2 6.4 %collective-permute-start.4 = (bf16[28,4,256]{2,0,1:T(8,128)(2,1)S(1)}, bf16[28,4,256]{2,0,1:T(8,128)(2,1)S(1)}, u32[]{:S(2)}, u32[]{:S(2)}) collective-permute-start(bf16[28,4,256]{2,0,1:T(8,128)(2,1)S(1)} %collective-permute-done.3), channel_id=1, source_target_pairs={{0,1},{1,2},{2,3},{3,4},{4,5},{5,6},{6,7},{7,8},{8,9},{9,10},{10,1... | collective-permute-start | bytes 172040 | tf_op jit(solution)/shard_map/ppermute | solution.py:82
  56.2 6.4 %collective-permute-start.11 = (bf16[28,4,256]{2,0,1:T(8,128)(2,1)S(1)}, bf16[28,4,256]{2,0,1:T(8,128)(2,1)S(1)}, u32[]{:S(2)}, u32[]{:S(2)}) collective-permute-start(bf16[28,4,256]{2,0,1:T(8,128)(2,1)S(1)} %collective-permute-done.10), channel_id=1, source_target_pairs={{0,15},{1,0},{2,1},{3,2},{4,3},{5,4},{6,5},{7,6},{8,7},{9,8},{10,9... | collective-permute-start | bytes 172040 | tf_op jit(solution)/shard_map/ppermute | solution.py:85
  62.6 6.4 %collective-permute-start.5 = (bf16[28,4,256]{2,0,1:T(8,128)(2,1)S(1)}, bf16[28,4,256]{2,0,1:T(8,128)(2,1)S(1)}, u32[]{:S(2)}, u32[]{:S(2)}) collective-permute-start(bf16[28,4,256]{2,0,1:T(8,128)(2,1)S(1)} %collective-permute-done.4), channel_id=1, source_target_pairs={{0,1},{1,2},{2,3},{3,4},{4,5},{5,6},{6,7},{7,8},{8,9},{9,10},{10,1... | collective-permute-start | bytes 172040 | tf_op jit(solution)/shard_map/ppermute | solution.py:82
  62.6 6.4 %collective-permute-start.12 = (bf16[28,4,256]{2,0,1:T(8,128)(2,1)S(1)}, bf16[28,4,256]{2,0,1:T(8,128)(2,1)S(1)}, u32[]{:S(2)}, u32[]{:S(2)}) collective-permute-start(bf16[28,4,256]{2,0,1:T(8,128)(2,1)S(1)} %collective-permute-done.11), channel_id=1, source_target_pairs={{0,15},{1,0},{2,1},{3,2},{4,3},{5,4},{6,5},{7,6},{8,7},{9,8},{10,9... | collective-permute-start | bytes 172040 | tf_op jit(solution)/shard_map/ppermute | solution.py:85
  69.0 6.4 %collective-permute-start.6 = (bf16[28,4,256]{2,0,1:T(8,128)(2,1)S(1)}, bf16[28,4,256]{2,0,1:T(8,128)(2,1)S(1)}, u32[]{:S(2)}, u32[]{:S(2)}) collective-permute-start(bf16[28,4,256]{2,0,1:T(8,128)(2,1)S(1)} %collective-permute-done.5), channel_id=1, source_target_pairs={{0,1},{1,2},{2,3},{3,4},{4,5},{5,6},{6,7},{7,8},{8,9},{9,10},{10,1... | collective-permute-start | bytes 172040 | tf_op jit(solution)/shard_map/ppermute | solution.py:82
  69.0 6.4 %collective-permute-start.13 = (bf16[28,4,256]{2,0,1:T(8,128)(2,1)S(1)}, bf16[28,4,256]{2,0,1:T(8,128)(2,1)S(1)}, u32[]{:S(2)}, u32[]{:S(2)}) collective-permute-start(bf16[28,4,256]{2,0,1:T(8,128)(2,1)S(1)} %collective-permute-done.12), channel_id=1, source_target_pairs={{0,15},{1,0},{2,1},{3,2},{4,3},{5,4},{6,5},{7,6},{8,7},{9,8},{10,9... | collective-permute-start | bytes 172040 | tf_op jit(solution)/shard_map/ppermute | solution.py:85
  75.4 6.4 %collective-permute-start.7 = (bf16[28,4,256]{2,0,1:T(8,128)(2,1)S(1)}, bf16[28,4,256]{2,0,1:T(8,128)(2,1)S(1)}, u32[]{:S(2)}, u32[]{:S(2)}) collective-permute-start(bf16[28,4,256]{2,0,1:T(8,128)(2,1)S(1)} %collective-permute-done.6), channel_id=1, source_target_pairs={{0,1},{1,2},{2,3},{3,4},{4,5},{5,6},{6,7},{7,8},{8,9},{9,10},{10,1... | collective-permute-start | bytes 172040 | tf_op jit(solution)/shard_map/ppermute | solution.py:82
  75.4 6.4 %collective-permute-start.14 = (bf16[28,4,256]{2,0,1:T(8,128)(2,1)S(1)}, bf16[28,4,256]{2,0,1:T(8,128)(2,1)S(1)}, u32[]{:S(2)}, u32[]{:S(2)}) collective-permute-start(bf16[28,4,256]{2,0,1:T(8,128)(2,1)S(1)} %collective-permute-done.13), channel_id=1, source_target_pairs={{0,15},{1,0},{2,1},{3,2},{4,3},{5,4},{6,5},{7,6},{8,7},{9,8},{10,9... | collective-permute-start | bytes 172040 | tf_op jit(solution)/shard_map/ppermute | solution.py:85
  81.8 6.4 %collective-permute-start.8 = (bf16[28,4,256]{2,0,1:T(8,128)(2,1)S(1)}, bf16[28,4,256]{2,0,1:T(8,128)(2,1)S(1)}, u32[]{:S(2)}, u32[]{:S(2)}) collective-permute-start(bf16[28,4,256]{2,0,1:T(8,128)(2,1)S(1)} %collective-permute-done.7), channel_id=1, source_target_pairs={{0,1},{1,2},{2,3},{3,4},{4,5},{5,6},{6,7},{7,8},{8,9},{9,10},{10,1... | collective-permute-start | bytes 172040 | tf_op jit(solution)/shard_map/ppermute | solution.py:82
  81.9 6.5 %collective-permute-start.15 = (bf16[28,4,256]{2,0,1:T(8,128)(2,1)S(1)}, bf16[28,4,256]{2,0,1:T(8,128)(2,1)S(1)}, u32[]{:S(2)}, u32[]{:S(2)}) collective-permute-start(bf16[28,4,256]{2,0,1:T(8,128)(2,1)S(1)} %collective-permute-done.14), channel_id=1, source_target_pairs={{0,15},{1,0},{2,1},{3,2},{4,3},{5,4},{6,5},{7,6},{8,7},{9,8},{10,9... | collective-permute-start | bytes 172040 | tf_op jit(solution)/shard_map/ppermute | solution.py:85
  88.2 6.4 %collective-permute-start.9 = (bf16[28,4,256]{2,0,1:T(8,128)(2,1)S(1)}, bf16[28,4,256]{2,0,1:T(8,128)(2,1)S(1)}, u32[]{:S(2)}, u32[]{:S(2)}) collective-permute-start(bf16[28,4,256]{2,0,1:T(8,128)(2,1)S(1)} %collective-permute-done.8), channel_id=1, source_target_pairs={{0,1},{1,2},{2,3},{3,4},{4,5},{5,6},{6,7},{7,8},{8,9},{9,10},{10,1... | collective-permute-start | bytes 172040 | tf_op jit(solution)/shard_map/ppermute | solution.py:82
  88.3 6.5 %collective-permute-start.16 = (bf16[28,4,256]{2,0,1:T(8,128)(2,1)S(1)}, bf16[28,4,256]{2,0,1:T(8,128)(2,1)S(1)}, u32[]{:S(2)}, u32[]{:S(2)}) collective-permute-start(bf16[28,4,256]{2,0,1:T(8,128)(2,1)S(1)} %collective-permute-done.15), channel_id=1, source_target_pairs={{0,15},{1,0},{2,1},{3,2},{4,3},{5,4},{6,5},{7,6},{8,7},{9,8},{10,9... | collective-permute-start | bytes 172040 | tf_op jit(solution)/shard_map/ppermute | solution.py:85
  124.7 1.0 copy-start
Sparse Core Ops, SparseCore 0:
  125.8 20.4 reduce-scatter.1
